TPU v7x, 256 devices: a whole 4x4x8 slice. The times are simulated.
256 devices in a mesh: pipe: 4 (over z_lo), expert: 64 (over x, z_hi, y, core).
Axes of the slice: x: 4, y: 4, z: 8 (z_hi: 2, z_lo: 4; z = z_hi * 4 + z_lo), core: 2. Of those that a mesh axis runs over, the one named last changes fastest.
Arguments:
- forward_input: bfloat16 [4, 8192, 2048], P('pipe', 'expert'), may hold values from -6 to 6
- queries: bfloat16 [4, 8192, 2048], P('pipe', 'expert'), may hold values from -100 to 100
- new_keys: bfloat16 [4, 8192, 256], P('pipe', 'expert'), may hold values from -6 to 6
- new_values: bfloat16 [4, 8192, 256], P('pipe', 'expert'), may hold values from -6 to 6
- cache_keys: bfloat16 [4, 8192, 256], P('pipe', 'expert'), may hold values from -6 to 6
- cache_values: bfloat16 [4, 8192, 256], P('pipe', 'expert'), may hold values from -6 to 6
- context_lengths: int32 [4, 64], P('pipe', 'expert'), may hold values from 1 to 128
- norm_gain: float32 [4, 2048], P('pipe'), may hold values from 0.5 to 1.5
- router: bfloat16 [4, 2048, 64], P('pipe'), may hold values from -0.125 to 0.125
- gate_weight: bfloat16 [4, 64, 2048, 768], P('pipe', 'expert'), may hold values from -0.125 to 0.125
- up_weight: bfloat16 [4, 64, 2048, 768], P('pipe', 'expert'), may hold values from -0.125 to 0.125
- down_weight: bfloat16 [4, 64, 768, 2048], P('pipe', 'expert'), may hold values from -0.21875 to 0.21875
- forward_ids: int32 [4, 8192, 4], P('pipe', 'expert'), may hold values from 0 to 63, all different within a row; in each aligned block of 128 rows (0 to 127, 128 to 255, ..., all dimensions but the last counted through in order) at most 9 rows name the same one
- backward_input: bfloat16 [4, 8192, 2048], P('pipe', 'expert'), may hold values from -6 to 6
- backward_ids: int32 [4, 8192, 4], P('pipe', 'expert'), may hold values from 0 to 63, all different within a row; in each aligned block of 128 rows (0 to 127, 128 to 255, ..., all dimensions but the last counted through in order) at most 9 rows name the same one
- output_grad: bfloat16 [4, 8192, 2048], P('pipe', 'expert'), may hold values from -16 to 16
Outputs:
- forward_output: bfloat16 [4, 8192, 2048], P('pipe', 'expert')
- input_grad: bfloat16 [4, 8192, 2048], P('pipe', 'expert')
- router_grad: float32 [4, 2048, 64], P('pipe', 'expert')
- gain_grad: float32 [4, 2048], P('pipe', 'expert')
Inputs may be any that keep to these rules, and one draw needn't show every extreme that they name: `forward_ids`: each row names 4 different experts; in the 128 rows of one device no expert is named more than 9 times, and on some devices one is named exactly 9 times. `backward_ids`: each row names 4 different experts; in the 128 rows of one device no expert is named more than 9 times, and on some devices one is named exactly 9 times.
All inputs are finite; a program needn't handle non-finite values.
Results may differ from a plain program's by a relative error of at most 0.012.
Values may be sent and summed in bfloat16 or wider, within the bound.
No kernel may reach another device: no remote copies, remote signals or barrier semaphores. Data moves between devices by JAX's collectives and lax.ppermute only.
A program may use at most 128 MiB of HBM per device.

v0:
```python
import math

import jax
import jax.numpy as jnp
from jax import lax
from jax.sharding import PartitionSpec as P

HEADS = 16
KV_HEADS = 2
HEAD_DIM = 128


epsilon = 1e-06
far_below = -1e30


def sent_together(arrays, axis, split_dim, concat_dim, along):
    both = jnp.concatenate(arrays, axis=along)
    result, at, outs = (
        lax.all_to_all(both, axis, split_axis=split_dim, concat_axis=concat_dim, tiled=True),
        0,
        [],
    )
    for a in arrays:
        outs.append(lax.slice_in_dim(result, at, at + a.shape[along], axis=along))
        at += a.shape[along]
    return tuple(outs)


def side_by_side(arrays, axis, split_dim, concat_dim, along):
    widths = [math.prod(a.shape[along:]) for a in arrays]
    both = jnp.concatenate(
        [a.reshape(*a.shape[:along], w) for a, w in zip(arrays, widths)], axis=along
    )
    result = lax.all_to_all(both, axis, split_axis=split_dim, concat_axis=concat_dim, tiled=True)
    tiles = jnp.split(result, [sum(widths[:k]) for k in range(1, len(widths))], axis=along)
    return tuple(
        (b.reshape(*result.shape[:along], *a.shape[along:]) for a, b in zip(arrays, tiles))
    )


def split_up(x, dim, devices):
    dims = x.shape
    tiles = x.reshape(*dims[:dim], devices, dims[dim] // devices, *dims[dim + 1 :])
    return jnp.moveaxis(tiles, dim, 0)


def summed_on_arrival(x, axis, dim):
    devices = lax.axis_size(axis)
    tiles = lax.all_to_all(split_up(x, dim, devices), axis, 0, 0, tiled=True)
    return jnp.sum(tiles, axis=0)


def side_by_side_2(arrays, axis, dim, along):
    widths = [math.prod(a.shape[along:]) for a in arrays]
    both = jnp.concatenate(
        [a.reshape(*a.shape[:along], w) for a, w in zip(arrays, widths)], axis=along
    )
    result = summed_on_arrival(both, axis, dim)
    tiles = jnp.split(result, [sum(widths[:k]) for k in range(1, len(widths))], axis=along)
    return tuple(
        (b.reshape(*result.shape[:along], *a.shape[along:]) for a, b in zip(arrays, tiles))
    )


def extended(x, sides, width):
    for axis, dim in sides:
        devices, length = (lax.axis_size(axis), x.shape[dim])
        up = [(i, (i + 1) % devices) for i in range(devices)]
        down = [(j, i) for i, j in up]
        last = lax.slice_in_dim(x, length - width, length, axis=dim)
        leading = lax.slice_in_dim(x, 0, width, axis=dim)
        before = lax.ppermute(last, axis, up)
        after = lax.ppermute(leading, axis, down)
        x = jnp.concatenate([before, x, after], axis=dim)
    return x


def normalize(resid, gain):
    wide = resid.astype(jnp.float32)
    inv_rms = lax.rsqrt(jnp.mean(wide * wide, axis=-1, keepdims=True) + epsilon)
    return (wide, inv_rms, (wide * inv_rms * gain).astype(jnp.bfloat16))


def routing(normed, expert_ids, table):
    logits = jnp.dot(normed, table, preferred_element_type=jnp.float32)
    selects = expert_ids[:, :, None] == jnp.arange(table.shape[1], dtype=jnp.int32)
    chosen = jnp.sum(jnp.where(selects, logits[:, None, :], 0.0), axis=-1)
    route_probs = 1.0 / jnp.sum(jnp.exp(chosen[:, None, :] - chosen[:, :, None]), axis=-1)
    return (route_probs, selects)


def place_slots(selects, capacity):
    counted = selects.reshape(-1, selects.shape[-1]).astype(jnp.int32)
    running = jnp.cumsum(counted, axis=0)
    slot_index = jnp.sum(counted * running, axis=-1) - 1
    owner = jnp.sum(counted * jnp.arange(selects.shape[-1], dtype=jnp.int32), axis=-1)
    return (owner * capacity + slot_index).reshape(selects.shape[0], selects.shape[1])


def pack_rows(source_rows, target, experts, capacity):
    buffer = jnp.zeros((experts * capacity, source_rows.shape[1]), source_rows.dtype)
    spread = jnp.broadcast_to(source_rows[:, None, :], target.shape + (source_rows.shape[1],))
    return buffer.at[target].set(spread).reshape(experts, capacity, source_rows.shape[1])


def unpack_rows(buffer, target):
    return buffer.reshape((-1,) + buffer.shape[2:])[target]


def gather_slots(received, per_device):
    shaped = received.reshape((-1, per_device) + received.shape[1:])
    return jnp.swapaxes(shaped, 0, 1).reshape((per_device, -1) + received.shape[2:])


def scatter_slots(result, sources):
    shaped = result.reshape((result.shape[0], sources, -1) + result.shape[2:])
    return jnp.swapaxes(shaped, 0, 1).reshape((-1,) + shaped.shape[2:])


def attention(queries, new_keys, new_values, cache_keys, cache_values, length):
    tokens = queries.shape[0]
    context = cache_keys.shape[0]
    key_rows = jnp.concatenate([cache_keys, new_keys], axis=0).reshape(-1, KV_HEADS, HEAD_DIM)
    value_rows = jnp.concatenate([cache_values, new_values], axis=0).reshape(-1, KV_HEADS, HEAD_DIM)
    grouped = queries.reshape(tokens, KV_HEADS, HEADS // KV_HEADS, HEAD_DIM)
    scores = jnp.einsum(
        "tkgd,skd->kgts", grouped, key_rows, preferred_element_type=jnp.float32
    ) * HEAD_DIM ** (-0.5)
    position = jnp.arange(key_rows.shape[0], dtype=jnp.int32)[None, :]
    query_pos = jnp.arange(tokens, dtype=jnp.int32)[:, None]
    visible = jnp.where(position < context, position < length, position - context <= query_pos)
    scores = jnp.where(visible, scores, far_below)
    row_max = jnp.max(scores, axis=-1, keepdims=True)
    lifted = jnp.exp(scores - row_max)
    attn_weights = (lifted / jnp.sum(lifted, axis=-1, keepdims=True)).astype(jnp.bfloat16)
    merged = jnp.einsum(
        "kgts,skd->tkgd", attn_weights, value_rows, preferred_element_type=jnp.float32
    )
    return merged.reshape(tokens, HEADS * HEAD_DIM).astype(jnp.bfloat16)


def expert_ahead(slot_rows, gate_matrix, up_matrix, down_matrix):
    gate_pre = jnp.einsum(
        "erd,edf->erf", slot_rows, gate_matrix, preferred_element_type=jnp.float32
    )
    up_pre = jnp.einsum("erd,edf->erf", slot_rows, up_matrix, preferred_element_type=jnp.float32)
    hidden = (gate_pre * jax.nn.sigmoid(gate_pre) * up_pre).astype(jnp.bfloat16)
    return jnp.einsum(
        "erf,efd->erd", hidden, down_matrix, preferred_element_type=jnp.float32
    ).astype(jnp.bfloat16)


def expert_behind(slot_rows, slot_grads, gate_matrix, up_matrix, down_matrix):
    gate_pre = jnp.einsum(
        "erd,edf->erf", slot_rows, gate_matrix, preferred_element_type=jnp.float32
    )
    up_pre = jnp.einsum("erd,edf->erf", slot_rows, up_matrix, preferred_element_type=jnp.float32)
    sigmoid_gate = jax.nn.sigmoid(gate_pre)
    gate_act = gate_pre * sigmoid_gate
    hidden = (gate_act * up_pre).astype(jnp.bfloat16)
    down_grad = jnp.einsum(
        "erd,efd->erf", slot_grads, down_matrix, preferred_element_type=jnp.float32
    )
    weight_grad = jnp.sum(hidden.astype(jnp.float32) * down_grad, axis=-1).astype(jnp.bfloat16)
    slope_act = sigmoid_gate * (1.0 + gate_pre * (1.0 - sigmoid_gate))
    gate_grad = (down_grad * up_pre * slope_act).astype(jnp.bfloat16)
    up_grad = (down_grad * gate_act).astype(jnp.bfloat16)
    slot_back = jnp.einsum(
        "erf,edf->erd", gate_grad, gate_matrix, preferred_element_type=jnp.float32
    )
    slot_back = slot_back + jnp.einsum(
        "erf,edf->erd", up_grad, up_matrix, preferred_element_type=jnp.float32
    )
    return (slot_back.astype(jnp.bfloat16), weight_grad)


def body(
    forward_input,
    queries,
    new_keys,
    new_values,
    cache_keys,
    cache_values,
    context_lengths,
    norm_gain,
    router,
    gate_weight,
    up_weight,
    down_weight,
    forward_ids,
    backward_input,
    backward_ids,
    output_grad,
):
    tokens = forward_input.shape[1]
    experts = router.shape[2]
    fan_out = forward_ids.shape[2]
    per_device = gate_weight.shape[1]
    sources = lax.axis_size("expert")
    capacity = max(2, tokens * fan_out // experts + max(1, tokens * fan_out // (8 * experts)))
    gain = norm_gain[0]
    table = router[0]
    gate_local = gate_weight[0]
    up_local = up_weight[0]
    down_local = down_weight[0]
    mixed = attention(
        queries[0],
        new_keys[0],
        new_values[0],
        cache_keys[0],
        cache_values[0],
        context_lengths[0, 0],
    )
    resid_ahead = (forward_input[0].astype(jnp.float32) + mixed.astype(jnp.float32)).astype(
        jnp.bfloat16
    )
    ahead_wide, ahead_inv, ahead_normed = normalize(resid_ahead, gain)
    ahead_probs, ahead_selects = routing(ahead_normed, forward_ids[0], table)
    ahead_target = place_slots(ahead_selects, capacity)
    ahead_buffer = pack_rows(ahead_normed, ahead_target, experts, capacity)
    behind_wide, behind_inv, behind_normed = normalize(backward_input[0], gain)
    behind_probs, behind_selects = routing(behind_normed, backward_ids[0], table)
    behind_target = place_slots(behind_selects, capacity)
    rows_buffer = pack_rows(behind_normed, behind_target, experts, capacity)
    grads_buffer = pack_rows(output_grad[0], behind_target, experts, capacity)
    arrived, behind_rows, behind_grads = sent_together(
        (ahead_buffer, rows_buffer, grads_buffer), "expert", 0, 0, 1
    )
    produced = scatter_slots(
        expert_ahead(gather_slots(arrived, per_device), gate_local, up_local, down_local), sources
    )
    slot_back, slot_weight = expert_behind(
        gather_slots(behind_rows, per_device),
        gather_slots(behind_grads, per_device),
        gate_local,
        up_local,
        down_local,
    )
    returned, input_back, weight_back = side_by_side(
        (produced, scatter_slots(slot_back, sources), scatter_slots(slot_weight, sources)),
        "expert",
        0,
        0,
        2,
    )
    ahead_rows = unpack_rows(returned, ahead_target).astype(jnp.float32)
    ahead_output = (ahead_wide + jnp.sum(ahead_probs[:, :, None] * ahead_rows, axis=1)).astype(
        jnp.bfloat16
    )
    input_rows = unpack_rows(input_back, behind_target).astype(jnp.float32)
    weight_rows = weight_back.reshape(-1)[behind_target].astype(jnp.float32)
    normed_grad = jnp.sum(behind_probs[:, :, None] * input_rows, axis=1)
    logit_terms = behind_probs * (
        weight_rows - jnp.sum(behind_probs * weight_rows, axis=-1, keepdims=True)
    )
    logit_grad = jnp.sum(jnp.where(behind_selects, logit_terms[:, :, None], 0.0), axis=1).astype(
        jnp.bfloat16
    )
    normed_grad = normed_grad + jnp.dot(logit_grad, table.T, preferred_element_type=jnp.float32)
    grad_factor = (tokens * sources) ** (-0.5)
    router_term = (
        jnp.dot(behind_normed.T, logit_grad, preferred_element_type=jnp.float32) * grad_factor
    )
    scaled_grad = normed_grad * gain
    resid_grad = behind_inv * (
        scaled_grad
        - behind_wide
        * behind_inv
        * behind_inv
        * jnp.mean(scaled_grad * behind_wide, axis=-1, keepdims=True)
    )
    gain_term = jnp.sum(normed_grad * behind_wide * behind_inv, axis=0) * grad_factor
    input_grad = (output_grad[0].astype(jnp.float32) + resid_grad).astype(jnp.bfloat16)
    router_part, gain_part = side_by_side_2((router_term, gain_term), "expert", 0, 1)
    crossing = extended(jnp.stack([input_grad, ahead_output]), (("pipe", 0),), 1)
    return (crossing[0][None], crossing[3][None], router_part[None], gain_part[None])


def solution(mesh):
    placed = (
        P("pipe", "expert", None),
        P("pipe", "expert", None),
        P("pipe", "expert", None),
        P("pipe", "expert", None),
        P("pipe", "expert", None),
        P("pipe", "expert", None),
        P("pipe", "expert"),
        P("pipe", None),
        P("pipe", None, None),
        P("pipe", "expert", None, None),
        P("pipe", "expert", None, None),
        P("pipe", "expert", None, None),
        P("pipe", "expert", None),
        P("pipe", "expert", None),
        P("pipe", "expert", None),
        P("pipe", "expert", None),
    )
    return jax.shard_map(
        body,
        mesh=mesh,
        in_specs=placed,
        out_specs=(
            P("pipe", "expert", None),
            P("pipe", "expert", None),
            P("pipe", "expert", None),
            P("pipe", "expert"),
        ),
        check_vma=False,
    )
```

profile of v0, /device:TPU:1, one launch (start us, length us, event | category | flops | bytes accessed | tf_op | source)
XLA Modules:
  0.0 660.0 jit_solution(9268469285581701670)
XLA Ops:
  31.3 6.4 scatter_custom_fusion.1
  51.7 6.3 scatter_custom_fusion
  70.0 6.3 scatter_custom_fusion.2
  81.0 7.0 %pad_maximum_fusion.1 = bf16[64,27,2048]{2,1,0:T(8,128)(2,1)S(1)} fusion(bf16[64,9,2048]{2,1,0:T(8,128)(2,1)} %reshape.464, bf16[64,9,2048]{2,1,0:T(8,128)(2,1)} %reshape.463, bf16[64,9,2048]{2,1,0:T(8,128)(2,1)} %reshape.461), kind=kLoop, calls=%fused_computation.8 | loop fusion | flops 21233664 | bytes 14155776 | tf_op jit(solution)/shard_map/concatenate | solution.py:18
  88.0 206.6 %all_to_all.15 = bf16[64,27,2048]{2,1,0:T(8,128)(2,1)S(1)} all-to-all(bf16[64,27,2048]{2,1,0:T(8,128)(2,1)S(1)} %pad_maximum_fusion.1), channel_id=1, replica_groups=mesh['pipe'=4,'expert'=64] {'expert'}, dimensions={0} | all-to-all | bytes 14155776 | tf_op jit(solution)/shard_map/all_to_all | solution.py:20
  294.6 5.6 fusion.111
  300.2 4.7 reshape.465
  304.9 4.7 reshape.470
  309.6 6.0 fusion.15
  322.0 9.0 %fusion.17 = bf16[576,2048]{1,0:T(8,128)(2,1)} fusion(bf16[1,1,768,2048]{3,2,1,0:T(8,128)(2,1)} %param.27, f32[576,768]{1,0:T(8,128)} %fusion.15, bf16[576,2048]{1,0:T(8,128)(2,1)} %reshape.465, bf16[1,1,2048,768]{3,2,1,0:T(8,128)(2,1)S(1)} %copy-done), kind=kOutput, calls=%fused_computation.28 | convolution fusion | flops 3627712512 | bytes 12779520 | tf_op jit(solution)/shard_map/erf,efd->erd/dot_general | solution.py:149
  335.6 5.1 reshape.469
  340.7 6.0 multiply_reduce_fusion.2
  354.7 7.2 %pad_maximum_fusion = bf16[64,9,4097]{2,1,0:T(8,128)(2,1)} fusion(bf16[64,9,1]{2,1,0:T(8,128)(2,1)S(1)} %convert_element_type.251, bf16[64,9,2048]{2,1,0:T(8,128)(2,1)} %reshape_transpose_reshape.10, bf16[64,9,2048]{2,1,0:T(8,128)(2,1)} %reshape_transpose_reshape.4), kind=kLoop, calls=%fused_computation.7 | loop fusion | flops 14159232 | bytes 9439488 | tf_op jit(solution)/shard_map/concatenate | solution.py:32
  361.8 5.6 all-to-all-start.1
  370.2 143.2 %all-to-all-done.1 = bf16[64,9,4097]{2,1,0:T(8,128)(2,1)} async-done(((bf16[64,9,4097]{2,1,0:T(8,128)(2,1)}), bf16[64,9,4097]{2,1,0:T(8,128)(2,1)}, u32[]{:S(2)}, u32[]{:S(2)}) %all-to-all-start.1) | async-done | bytes 4719776 | tf_op jit(solution)/shard_map/all_to_all | solution.py:35
  520.1 6.0 fusion.110
  532.9 4.8 reshape.532
  537.6 5.4 multiply_reduce_fusion
  548.1 6.9 %all-to-all-start.2 = ((f32[64,32,65]{2,1,0:T(8,128)}), f32[64,32,65]{2,1,0:T(8,128)}, u32[]{:S(2)}, u32[]{:S(2)}) async-start(f32[64,32,65]{2,1,0:T(8,128)} %pad_maximum_fusion.2), calls=%async_computation.2 | async-start | bytes 2097152 | tf_op jit(solution)/shard_map/all_to_all | solution.py:50
  556.2 52.7 %collective-permute-start.1 = (bf16[1,128,2048]{2,1,0:T(8,128)(2,1)}, bf16[1,128,2048]{2,1,0:T(8,128)(2,1)}, u32[]{:S(2)}, u32[]{:S(2)}) collective-permute-start(bf16[1,128,2048]{2,1,0:T(8,128)(2,1)} %fusion.72), channel_id=1, source_target_pairs={{64,0},{128,64},{192,128},{0,192},{65,1},{129,65},{193,129},{1,193... | collective-permute-start | bytes 1572872 | tf_op jit(solution)/shard_map/ppermute | solution.py:74
  615.8 4.8 reshape.531
  620.6 5.5 multiply_reduce_fusion.1
  626.4 12.0 %collective-permute-done.1 = bf16[1,128,2048]{2,1,0:T(8,128)(2,1)} collective-permute-done((bf16[1,128,2048]{2,1,0:T(8,128)(2,1)}, bf16[1,128,2048]{2,1,0:T(8,128)(2,1)}, u32[]{:S(2)}, u32[]{:S(2)}) %collective-permute-start.1) | collective-permute-done | bytes 524320 | tf_op jit(solution)/shard_map/ppermute | solution.py:74
  638.4 14.9 %collective-permute-done = bf16[1,128,2048]{2,1,0:T(8,128)(2,1)} collective-permute-done((bf16[1,128,2048]{2,1,0:T(8,128)(2,1)S(1)}, bf16[1,128,2048]{2,1,0:T(8,128)(2,1)}, u32[]{:S(2)}, u32[]{:S(2)}) %collective-permute-start) | collective-permute-done | bytes 524320 | tf_op jit(solution)/shard_map/ppermute | solution.py:73
  (146 shorter events, 115.1 us)
Async XLA Ops:
  0.6 318.2 %copy-start = (bf16[1,1,2048,768]{3,2,1,0:T(8,128)(2,1)S(1)}, bf16[1,1,2048,768]{3,2,1,0:T(8,128)(2,1)}, u32[]{:S(2)}) copy-start(bf16[1,1,2048,768]{3,2,1,0:T(8,128)(2,1)} %param.26) | copy-start | bytes 9437188
  15.8 5.6 copy-start.16
  18.4 3.0 copy-start.4
  18.4 3.0 copy-start.5
  18.4 3.0 copy-start.7
  309.6 6.0 copy-start.13
  309.6 6.0 copy-start.19
  340.7 6.1 copy-start.21
  346.8 2.4 copy-start.22
  361.8 7.3 %copy-start.15 = (bf16[1,2048,64]{1,2,0:T(8,128)(2,1)S(1)}, bf16[1,2048,64]{1,2,0:T(8,128)(2,1)}, u32[]{:S(2)}) copy-start(bf16[1,2048,64]{1,2,0:T(8,128)(2,1)} %param.24) | copy-start | bytes 786436
  361.8 151.6 %all-to-all-start.1 = ((bf16[64,9,4097]{2,1,0:T(8,128)(2,1)}), bf16[64,9,4097]{2,1,0:T(8,128)(2,1)}, u32[]{:S(2)}, u32[]{:S(2)}) async-start(bf16[64,9,4097]{2,1,0:T(8,128)(2,1)} %pad_maximum_fusion), calls=%async_computation.1 | async-start | bytes 17301504 | tf_op jit(solution)/shard_map/all_to_all | solution.py:35
  367.4 2.1 copy-start.18
  367.5 2.3 copy-start.6
  367.5 2.7 copy-start.17
  369.1 144.2 %copy-start.2 = (f32[1,128,2048]{2,1,0:T(8,128)}, f32[1,128,2048]{2,1,0:T(8,128)S(1)}, u32[]{:S(2)}) copy-start(f32[1,128,2048]{2,1,0:T(8,128)S(1)} %copy.61) | copy-start | bytes 3145732
  514.7 3.8 copy-start.11
  543.1 2.5 copy-start.12
  548.1 7.0 %copy-start.14 = (bf16[1,128,2048]{2,1,0:T(8,128)(2,1)S(1)}, bf16[1,128,2048]{2,1,0:T(8,128)(2,1)}, u32[]{:S(2)}) copy-start(bf16[1,128,2048]{2,1,0:T(8,128)(2,1)} %param.31) | copy-start | bytes 1572868
  548.1 105.2 %all-to-all-start.2 = ((f32[64,32,65]{2,1,0:T(8,128)}), f32[64,32,65]{2,1,0:T(8,128)}, u32[]{:S(2)}, u32[]{:S(2)}) async-start(f32[64,32,65]{2,1,0:T(8,128)} %pad_maximum_fusion.2), calls=%async_computation.2 | async-start | bytes 2097152 | tf_op jit(solution)/shard_map/all_to_all | solution.py:50
  556.2 82.2 %collective-permute-start.1 = (bf16[1,128,2048]{2,1,0:T(8,128)(2,1)}, bf16[1,128,2048]{2,1,0:T(8,128)(2,1)}, u32[]{:S(2)}, u32[]{:S(2)}) collective-permute-start(bf16[1,128,2048]{2,1,0:T(8,128)(2,1)} %fusion.72), channel_id=1, source_target_pairs={{64,0},{128,64},{192,128},{0,192},{65,1},{129,65},{193,129},{1,193... | collective-permute-start | bytes 1572872 | tf_op jit(solution)/shard_map/ppermute | solution.py:74
  620.6 5.5 copy-start.3
  620.6 5.6 copy-start.9
  626.1 33.6 %copy-start.1 = (bf16[1,1,2048,768]{3,2,1,0:T(8,128)(2,1)S(1)}, bf16[1,1,2048,768]{3,2,1,0:T(8,128)(2,1)}, u32[]{:S(2)}) copy-start(bf16[1,1,2048,768]{3,2,1,0:T(8,128)(2,1)} %param.26) | copy-start | bytes 9437188
  626.3 27.0 %collective-permute-start = (bf16[1,128,2048]{2,1,0:T(8,128)(2,1)S(1)}, bf16[1,128,2048]{2,1,0:T(8,128)(2,1)}, u32[]{:S(2)}, u32[]{:S(2)}) collective-permute-start(bf16[1,128,2048]{2,1,0:T(8,128)(2,1)S(1)} %fusion.50), channel_id=1, source_target_pairs={{0,64},{64,128},{128,192},{192,0},{1,65},{65,129},{129,193},{193,1... | collective-permute-start | bytes 1572872 | tf_op jit(solution)/shard_map/ppermute | solution.py:73
  (3 other events, 4.6 us)
where the time goes:
time: 668 us; the launch traced here: 660 us
  blocking collectives  207 us (31%)
  waiting for transfers between devices  170 us (25%)
  local copies, waits for them, and re-layouts  139 us (21%)
  starting transfers between devices  65.3 us (10%)
  matrix products  39.5 us (6%)
  other arithmetic  37.5 us (6%)
    all_to_all x1, blocking collectives, sent_together(): lax.all_to_all(both, axis, split_axis=split_dim, concat_axis=concat_dim,...  207 us
    all_to_all x1, waiting for transfers between devices, side_by_side(): lax.all_to_all(both, axis, split_axis=split_dim, concat_axis=concat_dim,...  143 us
    ppermute x1, starting transfers between devices, extended(): after = lax.ppermute(leading, axis, down)  52.7 us
    broadcast_in_dim x6, local copies, waits for them, and re-layouts, pack_rows(): jnp.broadcast_to(source_rows[:, None, :], target.shape + (source_rows.sha...  21.1 us
    scatter x3, local copies, waits for them, and re-layouts, pack_rows(): buffer.at[target].set(spread)  19.1 us
    ppermute x1, waiting for transfers between devices, extended(): before = lax.ppermute(last, axis, up)  14.9 us
    another operation x6, local copies, waits for them, and re-layouts  14.8 us
    reshape x3, local copies, waits for them, and re-layouts, pack_rows(): buffer.at[target].set(spread)  13.9 us
  transfers between devices with their start and end apart: 4, of which 3 were waited for; matrix products, arithmetic and copies ran while one was open for 3% of the time, Pallas kernels for 0%

commit v1 on v0

v1 whole, which is shorter than its diff:
```python
import jax
import jax.numpy as jnp
from jax import lax
from jax.sharding import Mesh, PartitionSpec as P

HEADS = 16
KV_HEADS = 2
HEAD_DIM = 128
D = 2048
FF = 768
EXPERTS = 64
MOST = 9
TOK = 128
PEERS = 32
SLOTS = PEERS * MOST
XY = ("x", "y", "core")
ALL = ("x", "zh", "y", "core")

epsilon = 1e-06
far_below = -1e30
bf16 = jnp.bfloat16
f32 = jnp.float32


def spread_out(x, axis=XY):
    return lax.all_to_all(x, axis, 0, 0, tiled=True)


def swapped(x):
    return lax.ppermute(x, "zh", [(0, 1), (1, 0)])


def moved(x, same, step):
    pairs = []
    for pipe in range(4):
        for zh in range(2):
            to = ((pipe + step) % 4) * 2 + (zh if same else 1 - zh)
            pairs.append((pipe * 2 + zh, to))
    return lax.ppermute(x, ("pipe", "zh"), pairs)


def normalize(x, gain):
    wide = x.astype(f32)
    inv_rms = lax.rsqrt(jnp.mean(wide * wide, axis=-1, keepdims=True) + epsilon)
    unit = wide * inv_rms
    return inv_rms, unit, (unit * gain).astype(bf16)


def chosen_of(ids):
    experts = jnp.arange(EXPERTS, dtype=jnp.int32)
    hit = ids[:, 0:1] == experts
    for k in range(1, ids.shape[1]):
        hit = hit | (ids[:, k : k + 1] == experts)
    return hit


def route_probs(normed, table, hit):
    logits = jnp.dot(normed, table, preferred_element_type=f32)
    logits = jnp.where(hit, logits, far_below)
    lifted = jnp.where(hit, jnp.exp(logits - jnp.max(logits, axis=-1, keepdims=True)), 0.0)
    return lifted / jnp.sum(lifted, axis=-1, keepdims=True)


def slot_tables(zh):
    p = jnp.arange(SLOTS, dtype=jnp.int32)
    d = p // MOST
    owner = (d // 8) * 16 + zh * 8 + d % 8
    pick = (owner[:, None] == jnp.arange(EXPERTS, dtype=jnp.int32)).astype(bf16)
    return pick, (p % MOST).astype(f32)[:, None]


def place(hit, pick, slot):
    row = lax.broadcasted_iota(jnp.int32, (TOK, TOK), 0)
    col = lax.broadcasted_iota(jnp.int32, (TOK, TOK), 1)
    before = (col < row).astype(bf16)
    rank = jnp.dot(before, hit.astype(bf16), preferred_element_type=f32)
    code = jnp.where(hit, rank + 1.0, 0.0).astype(bf16)
    spread = lax.dot_general(pick, code, (((1,), (1,)), ((), ())), preferred_element_type=f32)
    return (spread == slot + 1.0).astype(bf16)


def weighted(onehot, pick, probs):
    spread = lax.dot_general(
        pick, probs.astype(bf16), (((1,), (1,)), ((), ())), preferred_element_type=f32
    )
    return onehot * spread.astype(bf16)


def packed(onehot, rows):
    return jnp.dot(onehot, rows, preferred_element_type=f32).astype(bf16)


def summed(weights, rows):
    return lax.dot_general(weights, rows, (((0,), (0,)), ((), ())), preferred_element_type=f32)


def attention(queries, new_keys, new_values, cache_keys, cache_values, length):
    tokens = queries.shape[0]
    context = cache_keys.shape[0]
    key_rows = jnp.concatenate([cache_keys, new_keys], axis=0).reshape(-1, KV_HEADS, HEAD_DIM)
    value_rows = jnp.concatenate([cache_values, new_values], axis=0).reshape(-1, KV_HEADS, HEAD_DIM)
    grouped = queries.reshape(tokens, KV_HEADS, HEADS // KV_HEADS, HEAD_DIM)
    scores = jnp.einsum(
        "tkgd,skd->kgts", grouped, key_rows, preferred_element_type=f32
    ) * HEAD_DIM ** (-0.5)
    position = jnp.arange(key_rows.shape[0], dtype=jnp.int32)[None, :]
    query_pos = jnp.arange(tokens, dtype=jnp.int32)[:, None]
    visible = jnp.where(position < context, position < length, position - context <= query_pos)
    scores = jnp.where(visible, scores, far_below)
    row_max = jnp.max(scores, axis=-1, keepdims=True)
    lifted = jnp.exp(scores - row_max)
    attn_weights = (lifted / jnp.sum(lifted, axis=-1, keepdims=True)).astype(bf16)
    merged = jnp.einsum("kgts,skd->tkgd", attn_weights, value_rows, preferred_element_type=f32)
    return merged.reshape(tokens, HEADS * HEAD_DIM).astype(bf16)


def expert_ahead(rows, gate, up, down):
    gate_pre = jnp.dot(rows, gate, preferred_element_type=f32)
    up_pre = jnp.dot(rows, up, preferred_element_type=f32)
    hidden = (gate_pre * jax.nn.sigmoid(gate_pre) * up_pre).astype(bf16)
    return jnp.dot(hidden, down, preferred_element_type=f32).astype(bf16)


def expert_behind(rows, grads, gate, up, down):
    across = (((1,), (1,)), ((), ()))
    gate_pre = jnp.dot(rows, gate, preferred_element_type=f32)
    up_pre = jnp.dot(rows, up, preferred_element_type=f32)
    sig = jax.nn.sigmoid(gate_pre)
    act = gate_pre * sig
    hidden = (act * up_pre).astype(bf16)
    down_grad = lax.dot_general(grads, down, across, preferred_element_type=f32)
    weight_grad = jnp.sum(hidden.astype(f32) * down_grad, axis=-1)
    slope = sig * (1.0 + gate_pre * (1.0 - sig))
    gate_grad = (down_grad * up_pre * slope).astype(bf16)
    up_grad = (down_grad * act).astype(bf16)
    back = lax.dot_general(gate_grad, gate, across, preferred_element_type=f32)
    back = back + lax.dot_general(up_grad, up, across, preferred_element_type=f32)
    return back.astype(bf16), weight_grad.astype(bf16)


def body(
    forward_input,
    queries,
    new_keys,
    new_values,
    cache_keys,
    cache_values,
    context_lengths,
    norm_gain,
    router,
    gate_weight,
    up_weight,
    down_weight,
    forward_ids,
    backward_input,
    backward_ids,
    output_grad,
):
    zh = lax.axis_index("zh")
    gain = norm_gain[0]
    table = router[0]
    gate, up, down = gate_weight[0, 0], up_weight[0, 0], down_weight[0, 0]
    pick, slot = slot_tables(zh)

    back_x, back_g = backward_input[0], output_grad[0]
    ids = jnp.concatenate([backward_ids[0], forward_ids[0]], axis=1)
    ids_far = swapped(ids)
    x_far = swapped(back_x)
    g_far = swapped(back_g)

    def behind_side(x, g, chosen):
        hit = chosen_of(chosen)
        inv, unit, normed = normalize(x, gain)
        onehot = place(hit, pick, slot)
        probs = route_probs(normed, table, hit)
        sent = jnp.concatenate([packed(onehot, normed), packed(onehot, g)], axis=1)
        return inv, unit, normed, onehot, probs, sent.reshape(PEERS, MOST * 16, 256)

    inv_b, unit_b, normed_b, one_b, probs_b, sent_b = behind_side(back_x, back_g, ids[:, :4])
    got_b = spread_out(sent_b)
    inv_c, unit_c, normed_c, one_c, probs_c, sent_c = behind_side(x_far, g_far, ids_far[:, :4])
    got_c = spread_out(sent_c)

    mixed = attention(
        queries[0], new_keys[0], new_values[0], cache_keys[0], cache_values[0], context_lengths[0, 0]
    )
    resid = (forward_input[0].astype(f32) + mixed.astype(f32)).astype(bf16)
    resid_far = swapped(resid)

    def ahead_side(x, chosen):
        hit = chosen_of(chosen)
        _, _, normed = normalize(x, gain)
        onehot = place(hit, pick, slot)
        probs = route_probs(normed, table, hit)
        sent = packed(onehot, normed).reshape(PEERS, MOST * 8, 256)
        return weighted(onehot, pick, probs), sent

    mix_f, sent_f = ahead_side(resid, ids[:, 4:])
    mix_h, sent_h = ahead_side(resid_far, ids_far[:, 4:])
    got_f = spread_out(jnp.concatenate([sent_f, sent_h], axis=1))

    def behind_expert(got):
        both = got.reshape(SLOTS, 2 * D)
        back, grad = expert_behind(both[:, :D], both[:, D:], gate, up, down)
        return back.reshape(PEERS, MOST * 8, 256), grad.reshape(PEERS, MOST)

    back_b, grad_b = behind_expert(got_b)
    back_c, grad_c = behind_expert(got_c)
    extra = jnp.pad(
        jnp.concatenate([grad_b, grad_c], axis=1)[:, None, :], ((0, 0), (0, 7), (0, 256 - 2 * MOST))
    )
    home_b = spread_out(jnp.concatenate([back_b, back_c, extra], axis=1))

    made = expert_ahead(got_f.reshape(2 * SLOTS, D), gate, up, down)
    home_f = spread_out(made.reshape(PEERS, 2 * MOST * 8, 256))

    rows = MOST * 8
    sums_b = summed(weighted(one_b, pick, probs_b), home_b[:, :rows].reshape(SLOTS, D))
    sums_c = summed(weighted(one_c, pick, probs_c), home_b[:, rows : 2 * rows].reshape(SLOTS, D))
    grads = home_b[:, 2 * rows, : 2 * MOST]

    def grads_at(onehot, part):
        return summed(onehot * part.reshape(SLOTS, 1), pick)

    near = jnp.concatenate([grads_at(one_b, grads[:, :MOST]), grads_at(one_c, grads[:, MOST:])], axis=0)
    far = swapped(near)
    grad_of_b = near[:TOK] + far[TOK:]
    grad_of_c = near[TOK:] + far[:TOK]

    def logit_grads(probs, grad):
        return (probs * (grad - jnp.sum(probs * grad, axis=-1, keepdims=True))).astype(bf16)

    logit_b = logit_grads(probs_b, grad_of_b)
    logit_c = logit_grads(probs_c, grad_of_c)
    sums_b = sums_b + lax.dot_general(
        logit_b, table, (((1,), (1,)), ((), ())), preferred_element_type=f32
    )

    def through_norm(sums, inv, unit):
        scaled = sums * gain
        return inv * (scaled - unit * jnp.mean(scaled * unit, axis=-1, keepdims=True))

    own_b = (back_g.astype(f32) + through_norm(sums_b, inv_b, unit_b)).astype(bf16)
    own_c = through_norm(sums_c, inv_c, unit_c).astype(bf16)
    input_grad = (
        moved(own_b, True, -1).astype(f32) + moved(own_c, False, -1).astype(f32)
    ).astype(bf16)

    own_f = (
        resid.astype(f32) + summed(mix_f, home_f[:, :rows].reshape(SLOTS, D))
    ).astype(bf16)
    own_h = summed(mix_h, home_f[:, rows:].reshape(SLOTS, D)).astype(bf16)
    forward_output = (
        moved(own_f, True, 1).astype(f32) + moved(own_h, False, 1).astype(f32)
    ).astype(bf16)

    factor = 8192 ** (-0.5)
    gains = (jnp.sum(sums_b * unit_b, axis=0) + jnp.sum(sums_c * unit_c, axis=0)).reshape(4, 2, 256)
    mine = lax.dynamic_index_in_dim(gains, zh, 1, keepdims=False)
    theirs = lax.dynamic_index_in_dim(gains, 1 - zh, 1, keepdims=False)
    mine = (mine + swapped(theirs)).reshape(PEERS, 32, 1)
    normed_all = jnp.concatenate([normed_b, normed_c], axis=0).reshape(2 * TOK, 4, 2, 256)
    normed_all = lax.dynamic_index_in_dim(normed_all, zh, 2, keepdims=False).reshape(2 * TOK, D // 2)
    logit_all = jnp.concatenate([logit_b, logit_c], axis=0)
    router_part = summed(normed_all, logit_all).reshape(PEERS, 32, EXPERTS)
    shares = jnp.concatenate(
        [router_part, mine, jnp.zeros((PEERS, 32, 63), f32)], axis=2
    )
    total = jnp.sum(spread_out(shares), axis=0) * factor
    return (
        forward_output[None],
        input_grad[None],
        total[None, :, :EXPERTS],
        total[:, EXPERTS][None],
    )


def solution(mesh):
    grid = Mesh(mesh.devices.reshape(4, 4, 2, 4, 2), ("pipe", "x", "zh", "y", "core"))
    rows = P("pipe", ALL, None)
    placed = (
        rows,
        rows,
        rows,
        rows,
        rows,
        rows,
        P("pipe", ALL),
        P("pipe", None),
        P("pipe", None, None),
        P("pipe", ALL, None, None),
        P("pipe", ALL, None, None),
        P("pipe", ALL, None, None),
        rows,
        rows,
        rows,
        rows,
    )
    return jax.shard_map(
        body,
        mesh=grid,
        in_specs=placed,
        out_specs=(rows, rows, rows, P("pipe", ALL)),
        check_vma=False,
    )
```

time: 668 us -> 401 us (0.60)
  blocking collectives: 207 us -> 0 us
  waiting for transfers between devices: 170 us -> 64.2 us
  matrix products: 39.5 us -> 86.7 us
  local copies, waits for them, and re-layouts: 139 us -> 99.9 us
  starting transfers between devices: 65.3 us -> 101 us
    all_to_all x1 -> x0, blocking collectives: 207 us -> none  [sent_together(): lax.all_to_all(both, axis, split_axis=split_dim, concat_axis=concat_dim,...]
    all_to_all x2 -> x6, waiting for transfers between devices: 143 us -> 36.4 us  [spread_out(): return lax.all_to_all(x, axis, 0, 0, tiled=True)]
    dot_general x11 -> x34, matrix products: 33.4 us -> 80.5 us  [the longest x7 17.4 us: summed(): lax.dot_general(weights, rows, (((0,), (0,)), ((), ())), preferred_elemen...]
    reshape x5 -> x16, local copies, waits for them, and re-layouts: 20.8 us -> 58.3 us  [the longest x2 9.98 us: behind_expert(): both = got.reshape(SLOTS, 2 * D)]
    all_to_all x2 -> x6, starting transfers between devices: 12.5 us -> 47.7 us  [spread_out(): return lax.all_to_all(x, axis, 0, 0, tiled=True)]
    another operation x9 -> x0, local copies, waits for them, and re-layouts: 22.3 us -> none
    broadcast_in_dim x7 -> x2, local copies, waits for them, and re-layouts: 21.7 us -> 0.61 us  [the longest x1 0.61 us: body(): total[None, :, :EXPERTS]]
    scatter x3 -> x0, local copies, waits for them, and re-layouts: 19.1 us -> none  [pack_rows(): buffer.at[target].set(spread)]
  transfers between devices with their start and end apart: 4 -> 16, of which waited for: 3 -> 6; matrix products, arithmetic and copies ran while one was open for 3% -> 49% of each run, Pallas kernels for 0% -> 0%
where the time goes in v1:
time: 401 us; the launch traced here: 394 us
  starting transfers between devices  101 us (25%)
  local copies, waits for them, and re-layouts  99.9 us (25%)
  matrix products  86.7 us (22%)
  waiting for transfers between devices  64.2 us (16%)
  other arithmetic  40.2 us (10%)
    all_to_all x6, starting transfers between devices, spread_out(): return lax.all_to_all(x, axis, 0, 0, tiled=True)  47.7 us
    all_to_all x6, waiting for transfers between devices, spread_out(): return lax.all_to_all(x, axis, 0, 0, tiled=True)  36.4 us
    ppermute x4, starting transfers between devices, moved(): return lax.ppermute(x, ('pipe', 'zh'), pairs)  32.7 us
    ppermute x4, waiting for transfers between devices, moved(): return lax.ppermute(x, ('pipe', 'zh'), pairs)  27.7 us
    ppermute x6, starting transfers between devices, swapped(): return lax.ppermute(x, 'zh', [(0, 1), (1, 0)])  20.6 us
    dot_general x7, matrix products, summed(): lax.dot_general(weights, rows, (((0,), (0,)), ((), ())), preferred_elemen...  17.4 us
    unnamed x137, local copies, waits for them, and re-layouts  13.1 us
    dot_general x6, matrix products, packed(): return jnp.dot(onehot, rows, preferred_element_type=f32).astype(bf16)  11.4 us
  transfers between devices with their start and end apart: 16, of which 6 were waited for; matrix products, arithmetic and copies ran while one was open for 49% of the time, Pallas kernels for 0%

profile of v1, /device:TPU:1, one launch (start us, length us, event | category | flops | bytes accessed | tf_op | source)
XLA Modules:
  0.0 394.5 jit_solution(12976648478323952284)
XLA Ops:
  0.7 7.8 %collective-permute-start.4 = (bf16[128,2048]{1,0:T(8,128)(2,1)}, bf16[128,2048]{1,0:T(8,128)(2,1)}, u32[]{:S(2)}, u32[]{:S(2)}) collective-permute-start(bf16[128,2048]{1,0:T(8,128)(2,1)} %bitcast.208), channel_id=1, source_target_pairs={{0,8},{8,0},{1,9},{9,1},{2,10},{10,2},{3,11},{11,3},{4,12},{12,4},... | collective-permute-start | bytes 1572872 | tf_op jit(solution)/shard_map/ppermute | solution.py:30
  9.4 5.2 %collective-permute-start.5 = (bf16[128,2048]{1,0:T(8,128)(2,1)}, bf16[128,2048]{1,0:T(8,128)(2,1)}, u32[]{:S(2)}, u32[]{:S(2)}) collective-permute-start(bf16[128,2048]{1,0:T(8,128)(2,1)} %bitcast.212), channel_id=1, source_target_pairs={{0,8},{8,0},{1,9},{9,1},{2,10},{10,2},{3,11},{11,3},{4,12},{12,4},... | collective-permute-start | bytes 1572872 | tf_op jit(solution)/shard_map/ppermute | solution.py:30
  33.5 5.0 %reshape.260 = bf16[32,144,256]{2,1,0:T(8,128)(2,1)} reshape(bf16[288,4096]{1,0:T(8,128)(2,1)} %pad_maximum_fusion.1) | data formatting | bytes 4718592 | tf_op jit(solution)/shard_map/reshape | solution.py:177
  38.5 8.6 %all-to-all-start.2 = ((bf16[32,144,256]{2,1,0:T(8,128)(2,1)}), bf16[32,144,256]{2,1,0:T(8,128)(2,1)}, u32[]{:S(2)}, u32[]{:S(2)}) async-start(bf16[32,144,256]{2,1,0:T(8,128)(2,1)} %reshape.260), calls=%async_computation.2 | async-start | bytes 4718592 | tf_op jit(solution)/shard_map/all_to_all | solution.py:26
  63.0 5.0 %reshape.263 = bf16[32,144,256]{2,1,0:T(8,128)(2,1)} reshape(bf16[288,4096]{1,0:T(8,128)(2,1)} %pad_maximum_fusion.2) | data formatting | bytes 4718592 | tf_op jit(solution)/shard_map/reshape | solution.py:177
  68.0 10.4 %all-to-all-done.2 = bf16[32,144,256]{2,1,0:T(8,128)(2,1)} async-done(((bf16[32,144,256]{2,1,0:T(8,128)(2,1)}), bf16[32,144,256]{2,1,0:T(8,128)(2,1)}, u32[]{:S(2)}, u32[]{:S(2)}) %all-to-all-start.2) | async-done | bytes 2359328 | tf_op jit(solution)/shard_map/all_to_all | solution.py:26
  78.4 5.6 %all-to-all-start.3 = ((bf16[32,144,256]{2,1,0:T(8,128)(2,1)}), bf16[32,144,256]{2,1,0:T(8,128)(2,1)}, u32[]{:S(2)}, u32[]{:S(2)}) async-start(bf16[32,144,256]{2,1,0:T(8,128)(2,1)} %reshape.263), calls=%async_computation.3 | async-start | bytes 4718592 | tf_op jit(solution)/shard_map/all_to_all | solution.py:26
  103.8 5.0 %reshape.261 = bf16[288,4096]{1,0:T(8,128)(2,1)} reshape(bf16[32,144,256]{2,1,0:T(8,128)(2,1)} %all-to-all-done.2) | data formatting | bytes 4718592 | tf_op jit(solution)/shard_map/reshape | solution.py:203
  115.2 5.4 %all-to-all-start = ((bf16[32,144,256]{2,1,0:T(8,128)(2,1)}), bf16[32,144,256]{2,1,0:T(8,128)(2,1)}, u32[]{:S(2)}, u32[]{:S(2)}) async-start(bf16[32,144,256]{2,1,0:T(8,128)(2,1)} %pad_maximum_fusion), calls=%async_computation | async-start | bytes 4718592 | tf_op jit(solution)/shard_map/all_to_all | solution.py:26
  133.3 5.0 %reshape.264 = bf16[288,4096]{1,0:T(8,128)(2,1)} reshape(bf16[32,144,256]{2,1,0:T(8,128)(2,1)} %all-to-all-done.3) | data formatting | bytes 4718592 | tf_op jit(solution)/shard_map/reshape | solution.py:203
  142.5 9.3 %all-to-all-done = bf16[32,144,256]{2,1,0:T(8,128)(2,1)} async-done(((bf16[32,144,256]{2,1,0:T(8,128)(2,1)}), bf16[32,144,256]{2,1,0:T(8,128)(2,1)}, u32[]{:S(2)}, u32[]{:S(2)}) %all-to-all-start) | async-done | bytes 2359328 | tf_op jit(solution)/shard_map/all_to_all | solution.py:26
  156.8 5.9 %fusion.26 = f32[576,768]{1,0:T(8,128)} fusion(bf16[576,2048]{1,0:T(8,128)(2,1)} %reshape.256, bf16[1,1,2048,768]{3,2,1,0:T(8,128)(2,1)} %param.25), kind=kOutput, calls=%fused_computation.27 | convolution fusion | flops 1811939328 | bytes 7274496 | tf_op jit(solution)/shard_map/dot_general | solution.py:118
  162.7 9.0 %fusion.28 = bf16[576,2048]{1,0:T(8,128)(2,1)} fusion(bf16[1,1,768,2048]{3,2,1,0:T(8,128)(2,1)} %param.27, f32[576,768]{1,0:T(8,128)} %fusion.26, bf16[576,2048]{1,0:T(8,128)(2,1)} %reshape.256, bf16[1,1,2048,768]{3,2,1,0:T(8,128)(2,1)S(1)} %copy-done), kind=kOutput, calls=%fused_computation.29 | convolution fusion | flops 3627712512 | bytes 12779520 | tf_op jit(solution)/shard_map/dot_general | solution.py:121
  171.7 5.0 %reshape.257 = bf16[32,144,256]{2,1,0:T(8,128)(2,1)} reshape(bf16[576,2048]{1,0:T(8,128)(2,1)} %fusion.28) | data formatting | bytes 4718592 | tf_op jit(solution)/shard_map/reshape | solution.py:215
  176.7 14.1 %all-to-all-start.1 = ((bf16[32,144,256]{2,1,0:T(8,128)(2,1)}), bf16[32,144,256]{2,1,0:T(8,128)(2,1)}, u32[]{:S(2)}, u32[]{:S(2)}) async-start(bf16[32,144,256]{2,1,0:T(8,128)(2,1)} %reshape.257), calls=%async_computation.1 | async-start | bytes 4718592 | tf_op jit(solution)/shard_map/all_to_all | solution.py:26
  207.2 14.6 %all-to-all-done.1 = bf16[32,144,256]{2,1,0:T(8,128)(2,1)} async-done(((bf16[32,144,256]{2,1,0:T(8,128)(2,1)}), bf16[32,144,256]{2,1,0:T(8,128)(2,1)}, u32[]{:S(2)}, u32[]{:S(2)}) %all-to-all-start.1) | async-done | bytes 2359328 | tf_op jit(solution)/shard_map/all_to_all | solution.py:26
  221.9 5.3 %all-to-all-start.4 = ((bf16[32,152,256]{2,1,0:T(8,128)(2,1)}), bf16[32,152,256]{2,1,0:T(8,128)(2,1)}, u32[]{:S(2)}, u32[]{:S(2)}) async-start(bf16[32,152,256]{2,1,0:T(8,128)(2,1)} %fusion.43), calls=%async_computation.4 | async-start | bytes 4980736 | tf_op jit(solution)/shard_map/all_to_all | solution.py:26
  262.2 10.1 %collective-permute-start.2 = (bf16[128,2048]{1,0:T(8,128)(2,1)}, bf16[128,2048]{1,0:T(8,128)(2,1)}, u32[]{:S(2)}, u32[]{:S(2)}) collective-permute-start(bf16[128,2048]{1,0:T(8,128)(2,1)} %fusion.44), channel_id=1, source_target_pairs={{0,64},{8,72},{64,128},{72,136},{128,192},{136,200},{192,0},{200,8... | collective-permute-start | bytes 1572872 | tf_op jit(solution)/shard_map/ppermute | solution.py:39
  278.2 11.8 %collective-permute-start.3 = (bf16[128,2048]{1,0:T(8,128)(2,1)}, bf16[128,2048]{1,0:T(8,128)(2,1)}, u32[]{:S(2)}, u32[]{:S(2)}) collective-permute-start(bf16[128,2048]{1,0:T(8,128)(2,1)} %convolution_convert_fusion.6), channel_id=1, source_target_pairs={{0,72},{8,64},{64,136},{72,128},{128,200},{136,192},{192,8},{200,0... | collective-permute-start | bytes 1572872 | tf_op jit(solution)/shard_map/ppermute | solution.py:39
  326.5 5.0 %collective-permute-start.9 = (f32[4,256]{1,0:T(4,128)S(1)}, f32[4,256]{1,0:T(4,128)S(1)}, u32[]{:S(2)}, u32[]{:S(2)}) collective-permute-start(f32[4,256]{1,0:T(4,128)S(1)} %bitcast.234), channel_id=1, source_target_pairs={{0,8},{8,0},{1,9},{9,1},{2,10},{10,2},{3,11},{11,3},{4,12},{12,4},... | collective-permute-start | bytes 12296 | tf_op jit(solution)/shard_map/ppermute | solution.py:30
  337.8 8.7 %all-to-all-start.5 = ((f32[32,32,128]{2,1,0:T(8,128)}), f32[32,32,128]{2,1,0:T(8,128)}, u32[]{:S(2)}, u32[]{:S(2)}) async-start(f32[32,32,128]{2,1,0:T(8,128)} %maximum_maximum_fusion), calls=%async_computation.5 | async-start | bytes 1048576 | tf_op jit(solution)/shard_map/all_to_all | solution.py:26
  349.1 8.9 %collective-permute-start.8 = (bf16[128,2048]{1,0:T(8,128)(2,1)}, bf16[128,2048]{1,0:T(8,128)(2,1)}, u32[]{:S(2)}, u32[]{:S(2)}) collective-permute-start(bf16[128,2048]{1,0:T(8,128)(2,1)} %fusion.88), channel_id=1, source_target_pairs={{0,200},{8,192},{64,8},{72,0},{128,72},{136,64},{192,136},{200,128... | collective-permute-start | bytes 1572872 | tf_op jit(solution)/shard_map/ppermute | solution.py:39
  364.4 6.6 %collective-permute-done.8 = bf16[128,2048]{1,0:T(8,128)(2,1)} collective-permute-done((bf16[128,2048]{1,0:T(8,128)(2,1)}, bf16[128,2048]{1,0:T(8,128)(2,1)}, u32[]{:S(2)}, u32[]{:S(2)}) %collective-permute-start.8) | collective-permute-done | bytes 524320 | tf_op jit(solution)/shard_map/ppermute | solution.py:39
  371.0 21.1 %collective-permute-done.7 = bf16[128,2048]{1,0:T(8,128)(2,1)} collective-permute-done((bf16[128,2048]{1,0:T(8,128)(2,1)}, bf16[128,2048]{1,0:T(8,128)(2,1)}, u32[]{:S(2)}, u32[]{:S(2)}) %collective-permute-start.7) | collective-permute-done | bytes 524320 | tf_op jit(solution)/shard_map/ppermute | solution.py:39
  (261 shorter events, 193.7 us)
Async XLA Ops:
  0.6 119.9 %copy-start = (bf16[1,1,2048,768]{3,2,1,0:T(8,128)(2,1)S(1)}, bf16[1,1,2048,768]{3,2,1,0:T(8,128)(2,1)}, u32[]{:S(2)}) copy-start(bf16[1,1,2048,768]{3,2,1,0:T(8,128)(2,1)} %param.26) | copy-start | bytes 9437188
  0.6 21.6 %copy-start.14 = (bf16[1,128,256]{2,1,0:T(8,128)(2,1)S(1)}, bf16[1,128,256]{2,1,0:T(8,128)(2,1)}, u32[]{:S(2)}) copy-start(bf16[1,128,256]{2,1,0:T(8,128)(2,1)} %param.20) | copy-start | bytes 196612
  0.7 22.5 %copy-start.15 = (bf16[1,128,256]{2,1,0:T(8,128)(2,1)S(1)}, bf16[1,128,256]{2,1,0:T(8,128)(2,1)}, u32[]{:S(2)}) copy-start(bf16[1,128,256]{2,1,0:T(8,128)(2,1)} %param.18) | copy-start | bytes 196612
  0.7 22.7 %copy-start.16 = (bf16[1,128,256]{2,1,0:T(8,128)(2,1)S(1)}, bf16[1,128,256]{2,1,0:T(8,128)(2,1)}, u32[]{:S(2)}) copy-start(bf16[1,128,256]{2,1,0:T(8,128)(2,1)} %param.21) | copy-start | bytes 196612
  0.7 22.8 %copy-start.17 = (bf16[1,128,256]{2,1,0:T(8,128)(2,1)S(1)}, bf16[1,128,256]{2,1,0:T(8,128)(2,1)}, u32[]{:S(2)}) copy-start(bf16[1,128,256]{2,1,0:T(8,128)(2,1)} %param.19) | copy-start | bytes 196612
  0.7 26.4 %collective-permute-start.4 = (bf16[128,2048]{1,0:T(8,128)(2,1)}, bf16[128,2048]{1,0:T(8,128)(2,1)}, u32[]{:S(2)}, u32[]{:S(2)}) collective-permute-start(bf16[128,2048]{1,0:T(8,128)(2,1)} %bitcast.208), channel_id=1, source_target_pairs={{0,8},{8,0},{1,9},{9,1},{2,10},{10,2},{3,11},{11,3},{4,12},{12,4},... | collective-permute-start | bytes 1572872 | tf_op jit(solution)/shard_map/ppermute | solution.py:30
  9.2 48.2 %collective-permute-start = (s32[128,8]{0,1:T(8,128)S(1)}, s32[128,8]{0,1:T(8,128)S(1)}, u32[]{:S(2)}, u32[]{:S(2)}) collective-permute-start(s32[128,8]{0,1:T(8,128)S(1)} %pad_add_fusion), channel_id=1, source_target_pairs={{0,8},{8,0},{1,9},{9,1},{2,10},{10,2},{3,11},{11,3},{4,12},{12,4},... | collective-permute-start | bytes 12296 | tf_op jit(solution)/shard_map/ppermute | solution.py:30
  9.4 50.5 %collective-permute-start.5 = (bf16[128,2048]{1,0:T(8,128)(2,1)}, bf16[128,2048]{1,0:T(8,128)(2,1)}, u32[]{:S(2)}, u32[]{:S(2)}) collective-permute-start(bf16[128,2048]{1,0:T(8,128)(2,1)} %bitcast.212), channel_id=1, source_target_pairs={{0,8},{8,0},{1,9},{9,1},{2,10},{10,2},{3,11},{11,3},{4,12},{12,4},... | collective-permute-start | bytes 1572872 | tf_op jit(solution)/shard_map/ppermute | solution.py:30
  38.5 39.9 %all-to-all-start.2 = ((bf16[32,144,256]{2,1,0:T(8,128)(2,1)}), bf16[32,144,256]{2,1,0:T(8,128)(2,1)}, u32[]{:S(2)}, u32[]{:S(2)}) async-start(bf16[32,144,256]{2,1,0:T(8,128)(2,1)} %reshape.260), calls=%async_computation.2 | async-start | bytes 4718592 | tf_op jit(solution)/shard_map/all_to_all | solution.py:26
  55.0 38.4 %collective-permute-start.1 = (bf16[128,2048]{1,0:T(8,128)(2,1)}, bf16[128,2048]{1,0:T(8,128)(2,1)}, u32[]{:S(2)}, u32[]{:S(2)}) collective-permute-start(bf16[128,2048]{1,0:T(8,128)(2,1)} %get-tuple-element.11), channel_id=1, source_target_pairs={{0,8},{8,0},{1,9},{9,1},{2,10},{10,2},{3,11},{11,3},{4,12},{12,4},... | collective-permute-start | bytes 1572872 | tf_op jit(solution)/shard_map/ppermute | solution.py:30
  57.4 26.7 %copy-start.42 = (s32[128]{0:T(128)}, s32[128]{0:T(128)S(1)}, u32[]{:S(2)}) copy-start(s32[128]{0:T(128)S(1)} %get-tuple-element.35) | copy-start | bytes 1540
  57.4 26.7 %copy-start.43 = (s32[128]{0:T(128)}, s32[128]{0:T(128)S(1)}, u32[]{:S(2)}) copy-start(s32[128]{0:T(128)S(1)} %get-tuple-element.36) | copy-start | bytes 1540
  78.4 36.8 %all-to-all-start.3 = ((bf16[32,144,256]{2,1,0:T(8,128)(2,1)}), bf16[32,144,256]{2,1,0:T(8,128)(2,1)}, u32[]{:S(2)}, u32[]{:S(2)}) async-start(bf16[32,144,256]{2,1,0:T(8,128)(2,1)} %reshape.263), calls=%async_computation.3 | async-start | bytes 4718592 | tf_op jit(solution)/shard_map/all_to_all | solution.py:26
  91.7 135.4 %copy-start.41 = (f32[128]{0:T(128)}, f32[128]{0:T(128)S(1)}, u32[]{:S(2)}) copy-start(f32[128]{0:T(128)S(1)} %get-tuple-element.51) | copy-start | bytes 1540
  115.2 36.6 %all-to-all-start = ((bf16[32,144,256]{2,1,0:T(8,128)(2,1)}), bf16[32,144,256]{2,1,0:T(8,128)(2,1)}, u32[]{:S(2)}, u32[]{:S(2)}) async-start(bf16[32,144,256]{2,1,0:T(8,128)(2,1)} %pad_maximum_fusion), calls=%async_computation | async-start | bytes 4718592 | tf_op jit(solution)/shard_map/all_to_all | solution.py:26
  176.7 45.2 %all-to-all-start.1 = ((bf16[32,144,256]{2,1,0:T(8,128)(2,1)}), bf16[32,144,256]{2,1,0:T(8,128)(2,1)}, u32[]{:S(2)}, u32[]{:S(2)}) async-start(bf16[32,144,256]{2,1,0:T(8,128)(2,1)} %reshape.257), calls=%async_computation.1 | async-start | bytes 4718592 | tf_op jit(solution)/shard_map/all_to_all | solution.py:26
  221.9 68.1 %all-to-all-start.4 = ((bf16[32,152,256]{2,1,0:T(8,128)(2,1)}), bf16[32,152,256]{2,1,0:T(8,128)(2,1)}, u32[]{:S(2)}, u32[]{:S(2)}) async-start(bf16[32,152,256]{2,1,0:T(8,128)(2,1)} %fusion.43), calls=%async_computation.4 | async-start | bytes 4980736 | tf_op jit(solution)/shard_map/all_to_all | solution.py:26
  262.2 97.7 %collective-permute-start.2 = (bf16[128,2048]{1,0:T(8,128)(2,1)}, bf16[128,2048]{1,0:T(8,128)(2,1)}, u32[]{:S(2)}, u32[]{:S(2)}) collective-permute-start(bf16[128,2048]{1,0:T(8,128)(2,1)} %fusion.44), channel_id=1, source_target_pairs={{0,64},{8,72},{64,128},{72,136},{128,192},{136,200},{192,0},{200,8... | collective-permute-start | bytes 1572872 | tf_op jit(solution)/shard_map/ppermute | solution.py:39
  278.2 81.7 %collective-permute-start.3 = (bf16[128,2048]{1,0:T(8,128)(2,1)}, bf16[128,2048]{1,0:T(8,128)(2,1)}, u32[]{:S(2)}, u32[]{:S(2)}) collective-permute-start(bf16[128,2048]{1,0:T(8,128)(2,1)} %convolution_convert_fusion.6), channel_id=1, source_target_pairs={{0,72},{8,64},{64,136},{72,128},{128,200},{136,192},{192,8},{200,0... | collective-permute-start | bytes 1572872 | tf_op jit(solution)/shard_map/ppermute | solution.py:39
  304.4 13.0 %collective-permute-start.6 = (f32[256,64]{0,1:T(8,128)}, f32[256,64]{0,1:T(8,128)}, u32[]{:S(2)}, u32[]{:S(2)}) collective-permute-start(f32[256,64]{0,1:T(8,128)} %pad_maximum_fusion.4), channel_id=1, source_target_pairs={{0,8},{8,0},{1,9},{9,1},{2,10},{10,2},{3,11},{11,3},{4,12},{12,4},... | collective-permute-start | bytes 196616 | tf_op jit(solution)/shard_map/ppermute | solution.py:30
  326.5 8.0 %collective-permute-start.9 = (f32[4,256]{1,0:T(4,128)S(1)}, f32[4,256]{1,0:T(4,128)S(1)}, u32[]{:S(2)}, u32[]{:S(2)}) collective-permute-start(f32[4,256]{1,0:T(4,128)S(1)} %bitcast.234), channel_id=1, source_target_pairs={{0,8},{8,0},{1,9},{9,1},{2,10},{10,2},{3,11},{11,3},{4,12},{12,4},... | collective-permute-start | bytes 12296 | tf_op jit(solution)/shard_map/ppermute | solution.py:30
  337.8 24.1 %all-to-all-start.5 = ((f32[32,32,128]{2,1,0:T(8,128)}), f32[32,32,128]{2,1,0:T(8,128)}, u32[]{:S(2)}, u32[]{:S(2)}) async-start(f32[32,32,128]{2,1,0:T(8,128)} %maximum_maximum_fusion), calls=%async_computation.5 | async-start | bytes 1048576 | tf_op jit(solution)/shard_map/all_to_all | solution.py:26
  349.1 21.9 %collective-permute-start.8 = (bf16[128,2048]{1,0:T(8,128)(2,1)}, bf16[128,2048]{1,0:T(8,128)(2,1)}, u32[]{:S(2)}, u32[]{:S(2)}) collective-permute-start(bf16[128,2048]{1,0:T(8,128)(2,1)} %fusion.88), channel_id=1, source_target_pairs={{0,200},{8,192},{64,8},{72,0},{128,72},{136,64},{192,136},{200,128... | collective-permute-start | bytes 1572872 | tf_op jit(solution)/shard_map/ppermute | solution.py:39
  358.0 34.1 %collective-permute-start.7 = (bf16[128,2048]{1,0:T(8,128)(2,1)}, bf16[128,2048]{1,0:T(8,128)(2,1)}, u32[]{:S(2)}, u32[]{:S(2)}) collective-permute-start(bf16[128,2048]{1,0:T(8,128)(2,1)} %get-tuple-element.18), channel_id=1, source_target_pairs={{0,192},{8,200},{64,0},{72,8},{128,64},{136,72},{192,128},{200,136... | collective-permute-start | bytes 1572872 | tf_op jit(solution)/shard_map/ppermute | solution.py:39
  (56 other events, 407.8 us)
